TPU v7x, 256 devices: a whole 4x4x8 slice. The times are simulated.
256 devices in a mesh: replica: 32 (over z_lo, x, core), shard: 8 (over y, z_hi).
Axes of the slice: x: 4, y: 4, z: 8 (z_hi: 2, z_lo: 4; z = z_hi * 4 + z_lo), core: 2. Of those that a mesh axis runs over, the one named last changes fastest.
Arguments:
- normed: bfloat16 [65536, 8192], P(('replica', 'shard')), may hold values from -96 to 96
- out_grads: bfloat16 [65536, 1024], P(('replica', 'shard')), may hold values from -4 to 4
- weight: float32 [8192, 1024], P(('replica', 'shard')), may hold values from -6 to 6
- moment: float32 [8192, 1024], P(('replica', 'shard')), may hold values from -6 to 6
- variance: float32 [8192, 1024], P(('replica', 'shard')), may hold values from 0.5 to 8
Outputs:
- new_weight: float32 [8192, 1024], P(('replica', 'shard'))
- new_moment: float32 [8192, 1024], P(('replica', 'shard'))
- new_variance: float32 [8192, 1024], P(('replica', 'shard'))
All inputs are finite; a program needn't handle non-finite values.
Results may differ from a plain program's by a relative error of at most 0.002.
Values may be sent and summed in bfloat16 or wider, within the bound.
A program may use at most 128 MiB of HBM per device.

v0:
```python
import functools

import jax
import jax.numpy as jnp
from jax import lax
from jax.sharding import Mesh
from jax.sharding import PartitionSpec as P

TOK_DEV = 256
STEP = 10
REPLICA = ("replica_0", "replica_1", "replica_2")
SHARD = ("shard_0", "shard_1")
REPLICA_SHARD = ("replica_0", "replica_1", "replica_2", "shard_0", "shard_1")


def cut_along(shard, dim, devices):
    shape = shard.shape
    tiles = shard.reshape(*shape[:dim], devices, shape[dim] // devices, *shape[dim + 1 :])
    return jnp.moveaxis(tiles, dim, 0)


def sent_and_summed(shard, axis, dim):
    tiles = cut_along(shard, dim, lax.axis_size(axis))
    arrived = lax.all_to_all(tiles, axis, split_axis=0, concat_axis=0, tiled=True)
    return arrived.sum(axis=0)


def sum_in_two_steps(shard, axes, dim):
    far, near = axes
    tiles = cut_along(shard, dim, lax.axis_size(far))
    nearer = sent_and_summed(tiles, near, dim + 1)
    arrived = lax.all_to_all(nearer, far, split_axis=0, concat_axis=0, tiled=True)
    return arrived.sum(axis=0)


def by_axis(shard, axes):
    return functools.reduce(lax.psum, axes, shard)


def to_wire(values):
    return lax.optimization_barrier(values.astype(jnp.bfloat16)).astype(jnp.float32)


def shards(normed, out_grads, weight, moment, variance):
    tokens = normed.shape[0]
    width = normed.shape[1]
    columns = out_grads.shape[1]
    n_replica = lax.axis_size(REPLICA)
    n_shard = lax.axis_size(SHARD)
    own_rows = width // (n_replica * n_shard)
    group_rows = width // n_shard
    grid = normed.reshape(tokens, n_replica, n_shard, own_rows)
    mine = lax.all_to_all(grid, SHARD, split_axis=2, concat_axis=0, tiled=True)
    mine = mine.reshape(n_shard * tokens, group_rows)
    piece = lax.all_gather(out_grads, SHARD, axis=0, tiled=True)
    count = piece.shape[0] // TOK_DEV
    picked = mine.reshape(count, TOK_DEV, group_rows)
    parts = jnp.einsum(
        "ktd,ktc->kdc",
        picked,
        piece.reshape(count, TOK_DEV, columns),
        preferred_element_type=jnp.float32,
    )
    summed = jnp.sum(to_wire(parts), axis=0)
    grad = sum_in_two_steps(summed, (("replica_0", "replica_1"), "replica_2"), 0)
    squares = by_axis(jnp.sum(grad * grad), REPLICA_SHARD)
    limit = jnp.sqrt(jnp.float32(width * columns))
    clip = jnp.minimum(jnp.float32(1.0), limit / (jnp.sqrt(squares) + 1e-06))
    scaled = clip * grad
    new_moment = 0.9 * moment + 0.1 * scaled
    new_variance = 0.95 * variance + 0.05 * scaled * scaled
    first = new_moment / (1.0 - 0.9**STEP)
    second = new_variance / (1.0 - 0.95**STEP)
    new_weight = weight - 0.01 * (first / (jnp.sqrt(second) + 1e-08) + 0.1 * weight)
    return (new_weight, new_moment, new_variance)


def solution(mesh):
    split = Mesh(
        mesh.devices.reshape(4, 4, 2, 4, 2),
        ("replica_0", "replica_1", "replica_2", "shard_0", "shard_1"),
    )
    in_specs = (
        P(REPLICA_SHARD, None),
        P(REPLICA_SHARD, None),
        P(REPLICA_SHARD, None),
        P(REPLICA_SHARD, None),
        P(REPLICA_SHARD, None),
    )
    out_specs = (P(REPLICA_SHARD, None), P(REPLICA_SHARD, None), P(REPLICA_SHARD, None))
    return jax.shard_map(
        shards, mesh=split, in_specs=in_specs, out_specs=out_specs, check_vma=False
    )
```

profile of v0, /device:TPU:1, one launch (start us, length us, event | category | flops | bytes accessed | tf_op | source)
XLA Modules:
  0.0 326.8 jit_solution(12854906395120207865)
XLA Ops:
  7.2 0.0 all-gather.2.cloned.1.call-start
  7.2 0.7 all-gather.2.cloned.1.call-update
  7.9 6.4 %copy.16 = bf16[256,8192]{0,1:T(8,128)(2,1)} copy(bf16[256,8192]{1,0:T(8,128)(2,1)} %param.5) | data formatting | bytes 8388608 | tf_op args[0]
  14.3 4.7 %copy.17 = bf16[256,32,8,32]{0,3,1,2:T(8,128)(2,1)} copy(bf16[256,32,8,32]{0,3,2,1:T(8,128)(2,1)} %bitcast.13) | data formatting | bytes 8388608 | tf_op jit(solution)/shard_map/reshape | solution.py:52
  19.0 11.6 %all-to-all-start = ((bf16[256,32,8,32]{0,3,1,2:T(8,128)(2,1)}), bf16[256,32,8,32]{0,3,1,2:T(8,128)(2,1)}, u32[]{:S(2)}, u32[]{:S(2)}) async-start(bf16[256,32,8,32]{0,3,1,2:T(8,128)(2,1)} %copy.17), calls=%async_computation | async-start | bytes 8388608 | tf_op jit(solution)/shard_map/all_to_all | solution.py:53
  30.7 162.1 %all-gather.2.cloned.1.call-done = bf16[2048,1024]{1,0:T(8,128)(2,1)} async-done(((bf16[256,1024]{1,0:T(8,128)(2,1)}), bf16[2048,1024]{1,0:T(8,128)(2,1)}) %all-gather.2.cloned.1.call-update) | async-done | bytes 4194320 | tf_op jit(solution)/shard_map/all_gather | solution.py:55
  192.8 0.0 all-to-all-done
  192.8 10.9 %convolution_convert_fusion = bf16[8,1024,1024]{2,1,0:T(8,128)(2,1)} fusion(bf16[8,256,1024]{1,2,0:T(8,128)(2,1)} %bitcast.3, bf16[8,256,1024]{2,1,0:T(8,128)(2,1)} %bitcast.14), kind=kOutput, calls=%fused_computation.1 | convolution fusion | flops 4303355904 | bytes 25165824 | tf_op jit(solution)/shard_map/ktd,ktc->kdc/dot_general | solution.py:58
  203.7 7.2 %convert_reduce_fusion = f32[1024,1024]{1,0:T(8,128)S(1)} fusion(bf16[8,1024,1024]{2,1,0:T(8,128)(2,1)} %convolution_convert_fusion), kind=kLoop, calls=%fused_computation | loop fusion | flops 15728640 | bytes 20971520 | tf_op jit(solution)/shard_map/reduce_sum | solution.py:64
  210.9 0.6 copy.18
  211.5 8.9 %all_to_all.25 = f32[2,16,32,1024]{3,2,1,0:T(8,128)} all-to-all(f32[2,16,32,1024]{3,2,1,0:T(8,128)S(1)} %copy.18), channel_id=1, replica_groups=mesh['replica_0'=4,'replica_1'=4,'replica_2'=2,'shard_0'=4,'shard_1'=2] ..., dimensions={0} | all-to-all | bytes 8388608 | tf_op jit(solution)/shard_map/all_to_all | solution.py:24
  220.4 2.8 reduce_sum.37
  223.2 0.0 copy-start
  223.2 0.0 copy-start.1
  223.2 0.0 copy-start.2
  223.2 51.5 %all_to_all.26 = f32[16,32,1024]{2,1,0:T(8,128)} all-to-all(f32[16,32,1024]{2,1,0:T(8,128)S(1)} %reduce_sum.37), channel_id=1, replica_groups=mesh['replica_0'=4,'replica_1'=4,'replica_2'=2,'shard_0'=4,'shard_1'=2] ..., dimensions={0} | all-to-all | bytes 4194304 | tf_op jit(solution)/shard_map/all_to_all | solution.py:32
  274.7 1.7 reduce_sum.38
  276.4 0.6 multiply_reduce_fusion
  277.0 9.7 %psum.35 = f32[]{:T(128)} all-reduce(f32[]{:T(128)} %multiply_reduce_fusion), channel_id=1, replica_groups=mesh['replica_0'=4,'replica_1'=4,'replica_2'=2,'shard_0'=4,'shard_1'=2] ..., use_global_device_ids=true, to_apply=%region_4.0 | all-reduce | flops 1 | bytes 8 | tf_op jit(solution)/shard_map/psum | solution.py:37
  286.7 8.0 %psum.36 = f32[]{:T(128)} all-reduce(f32[]{:T(128)} %psum.35), channel_id=1, replica_groups=mesh['replica_0'=4,'replica_1'=4,'replica_2'=2,'shard_0'=4,'shard_1'=2] ..., use_global_device_ids=true, to_apply=%region_5.0 | all-reduce | flops 1 | bytes 8 | tf_op jit(solution)/shard_map/psum | solution.py:37
  294.7 8.2 %psum.37 = f32[]{:T(128)} all-reduce(f32[]{:T(128)} %psum.36), channel_id=1, replica_groups=mesh['replica_0'=4,'replica_1'=4,'replica_2'=2,'shard_0'=4,'shard_1'=2] ..., use_global_device_ids=true, to_apply=%region_6.0 | all-reduce | flops 1 | bytes 8 | tf_op jit(solution)/shard_map/psum | solution.py:37
  302.9 7.2 %psum.38 = f32[]{:T(128)} all-reduce(f32[]{:T(128)} %psum.37), channel_id=1, replica_groups=mesh['replica_0'=4,'replica_1'=4,'replica_2'=2,'shard_0'=4,'shard_1'=2] ..., use_global_device_ids=true, to_apply=%region_7.0 | all-reduce | flops 1 | bytes 8 | tf_op jit(solution)/shard_map/psum | solution.py:37
  310.0 8.3 %psum.39 = f32[]{:T(128)} all-reduce(f32[]{:T(128)} %psum.38), channel_id=1, replica_groups=mesh['replica_0'=4,'replica_1'=4,'replica_2'=2,'shard_0'=4,'shard_1'=2] ..., use_global_device_ids=true, to_apply=%region_8.0 | all-reduce | flops 1 | bytes 8 | tf_op jit(solution)/shard_map/psum | solution.py:37
  319.1 0.0 copy-done
  319.1 0.0 copy-done.1
  319.1 0.0 copy-done.2
  319.1 0.8 multiply_subtract_fusion
Async XLA Ops:
  7.2 185.6 %all-gather.2.cloned.1.call-start = ((), (), s32[]{:S(2)}) async-start(), calls=%async_computation.3 | async-start | bytes 4718592 | tf_op jit(solution)/shard_map/all_gather | solution.py:55
  19.0 173.8 %all-to-all-start = ((bf16[256,32,8,32]{0,3,1,2:T(8,128)(2,1)}), bf16[256,32,8,32]{0,3,1,2:T(8,128)(2,1)}, u32[]{:S(2)}, u32[]{:S(2)}) async-start(bf16[256,32,8,32]{0,3,1,2:T(8,128)(2,1)} %copy.17), calls=%async_computation | async-start | bytes 8388608 | tf_op jit(solution)/shard_map/all_to_all | solution.py:53
  223.2 95.9 %copy-start = (f32[32,1024]{1,0:T(8,128)S(1)}, f32[32,1024]{1,0:T(8,128)}, u32[]{:S(2)}) copy-start(f32[32,1024]{1,0:T(8,128)} %param.7) | copy-start | bytes 393220
  223.2 95.9 %copy-start.1 = (f32[32,1024]{1,0:T(8,128)S(1)}, f32[32,1024]{1,0:T(8,128)}, u32[]{:S(2)}) copy-start(f32[32,1024]{1,0:T(8,128)} %param.8) | copy-start | bytes 393220
  223.2 95.9 %copy-start.2 = (f32[32,1024]{1,0:T(8,128)S(1)}, f32[32,1024]{1,0:T(8,128)}, u32[]{:S(2)}) copy-start(f32[32,1024]{1,0:T(8,128)} %param.9) | copy-start | bytes 393220
Sparse Core Ops, SparseCore 0:
  10.6 182.1 all-gather.1
where the time goes:
time: 329 us; the launch traced here: 327 us
  waiting for transfers between devices  163 us (50%)
  blocking collectives  102 us (31%)
  between operations  14.8 us (4%)
  other arithmetic  13.1 us (4%)
  starting transfers between devices  11.7 us (4%)
  local copies, waits for them, and re-layouts  11.7 us (4%)
  matrix products  10.9 us (3%)
    all_gather x1, waiting for transfers between devices, shards(): piece = lax.all_gather(out_grads, SHARD, axis=0, tiled=True)  162 us
    all_to_all x1, blocking collectives, sum_in_two_steps(): lax.all_to_all(nearer, far, split_axis=0, concat_axis=0, tiled=True)  51.5 us
    psum x5, blocking collectives, by_axis(): return functools.reduce(lax.psum, axes, shard)  41.3 us
    all_to_all x1, starting transfers between devices, shards(): mine = lax.all_to_all(grid, SHARD, split_axis=2, concat_axis=0, tiled=True)  11.6 us
    dot_general x1, matrix products, shards(): jnp.einsum('ktd,ktc->kdc', picked, piece.reshape(count, TOK_DEV, columns)...  10.9 us
    all_to_all x1, blocking collectives, sent_and_summed(): lax.all_to_all(tiles, axis, split_axis=0, concat_axis=0, tiled=True)  8.88 us
    reduce_sum x1, other arithmetic, shards(): summed = jnp.sum(to_wire(parts), axis=0)  7.2 us
  transfers between devices with their start and end apart: 2, of which 1 were waited for; matrix products, arithmetic and copies ran while one was open for 3% of the time, Pallas kernels for 0%

commit v1 on v0

v1 whole, which is shorter than its diff:
```python
import jax
import jax.numpy as jnp
from jax import lax
from jax.experimental import pallas as pl
from jax.experimental.pallas import tpu as pltpu
from jax.sharding import Mesh
from jax.sharding import PartitionSpec as P

STEP = 10
AXES = ("z_lo", "x", "core", "y", "z_hi")
SIZES = (4, 4, 2, 4, 2)
MESH_ID = pl.DeviceIdType.MESH
F32, BF16 = jnp.float32, jnp.bfloat16
CX, CY, CZ = 384, 256, 384
BLOCK = 256
ROWS = 32
TOK = 256


class Sems:
    def __init__(self, send, recv):
        self.send, self.recv, self.used, self.sent = send, recv, 0, []

    def take(self):
        self.used += 1
        return self.send.at[self.used - 1], self.recv.at[self.used - 1]


class Ring:
    def __init__(self, n, me, device, view, length, landing, sems):
        self.n, self.me, self.device, self.view = n, me, device, view
        self.length, self.landing, self.sems = length, landing, sems
        self.copies = {}
        for way in (0, 1):
            for half in (0, 1):
                for hop in range(1, self.reach(way, half) + 1):
                    self.copies[way, half, hop] = self.copy(way, half, hop)

    def reach(self, way, half):
        return self.n // 2 if way == half else self.n // 2 - 1

    def slot(self, way, half, hop):
        return hop - 1 if half == 0 else self.reach(way, 0) + hop - 1

    def dest(self, way, hop):
        return lax.rem(self.me + (hop if way == 0 else self.n - hop), self.n)

    def copy(self, way, half, hop):
        send, recv = self.sems.take()
        return pltpu.make_async_remote_copy(
            src_ref=self.view(self.dest(way, hop), half),
            dst_ref=self.landing.at[way, self.slot(way, half, hop)],
            send_sem=send,
            recv_sem=recv,
            device_id=self.device(way),
            device_id_type=MESH_ID,
        )

    def send(self, way, half, hop):
        self.copies[way, half, hop].start()
        self.sems.sent.append(self.copies[way, half, hop])

    def first(self):
        for way in (0, 1):
            self.send(way, way, self.n // 2)

    def direct(self):
        for way in (0, 1):
            self.send(way, 1 - way, self.n // 2 - 1)

    def onward(self, far, hop):
        for way in (0, 1):
            half = way if far else 1 - way
            self.copies[way, half, hop + 1].wait_recv()
            target = self.view(self.dest(way, hop), half)
            came = self.landing.at[way, self.slot(way, half, hop + 1)]

            def add(i, _):
                target[i] = (target[i].astype(F32) + came[i].astype(F32)).astype(BF16)
                return 0

            lax.fori_loop(0, self.length, add, 0)
            self.send(way, half, hop)

    def last(self):
        for half in (0, 1):
            target = self.view(self.me, half)
            came = []
            for way in (0, 1):
                self.copies[way, half, 1].wait_recv()
                came.append(self.landing.at[way, self.slot(way, half, 1)])

            def add(i, _):
                total = target[i].astype(F32) + came[0][i].astype(F32)
                target[i] = (total + came[1][i].astype(F32)).astype(BF16)
                return 0

            lax.fori_loop(0, self.length, add, 0)


class Direct:
    def __init__(self, n, me, device, source, landing, sems):
        self.sems, self.copies = sems, []
        for off in range(1, n):
            dest = lax.rem(me + off, n)
            send, recv = sems.take()
            self.copies.append(
                pltpu.make_async_remote_copy(
                    src_ref=source(dest),
                    dst_ref=landing.at[off - 1],
                    send_sem=send,
                    recv_sem=recv,
                    device_id=device(dest),
                    device_id_type=MESH_ID,
                )
            )

    def start(self):
        for copy in self.copies:
            copy.start()
            self.sems.sent.append(copy)

    def arrive(self):
        for copy in self.copies:
            copy.wait_recv()


def kernel(
    normed, out_grads, out, lhs, rhs, px, py, pz, lx1, ly1, lz1, lx2, ly2, lz2, lx3, ly3, lz3,
    square, sqz, sqy, sqx, sqc, send_sem, recv_sem, load_sem, in_send, in_recv,
):
    x, y, core = lax.axis_index("x"), lax.axis_index("y"), lax.axis_index("core")
    z_lo, z_hi = lax.axis_index("z_lo"), lax.axis_index("z_hi")
    z = z_hi * 4 + z_lo
    other = 1 - core

    def at_x(i):
        return {"x": i}

    def at_y(i):
        return {"y": i}

    def at_z(i):
        return {"z_hi": i // 4, "z_lo": lax.rem(i, 4)}

    def step_on(place, n, me):
        return lambda way: place(lax.rem(me + (1 if way == 0 else n - 1), n))

    def columns(j, c):
        return pl.ds(pl.multiple_of((2 * j + c) * BLOCK, BLOCK), BLOCK)

    def own_load(j):
        return pltpu.make_async_copy(
            normed.at[:, columns(j, core)], lhs.at[j, pl.ds(0, TOK)], load_sem.at[j]
        )

    def partner_send(j):
        return pltpu.make_async_remote_copy(
            src_ref=normed.at[:, columns(j, other)],
            dst_ref=lhs.at[j, pl.ds(TOK, TOK)],
            send_sem=in_send.at[j],
            recv_sem=in_recv.at[j],
            device_id={"core": other},
            device_id_type=MESH_ID,
        )

    far_x = lax.rem(x + 2, 4)

    def block_a(i):
        return i * 4 + far_x

    def block_b(i):
        return z_lo * 4 + lax.rem(x + 3 + i, 4)

    def block_c(i):
        return lax.rem(z_lo + 1 + i // 3, 4) * 4 + lax.rem(x + 3 + lax.rem(i, 3), 4)

    groups = ((block_a, 4), (block_b, 3), (block_c, 9))

    grads_load = pltpu.make_async_copy(out_grads, rhs.at[pl.ds(0, TOK)], load_sem.at[16])
    grads_send = pltpu.make_async_remote_copy(
        src_ref=out_grads,
        dst_ref=rhs.at[pl.ds(TOK, TOK)],
        send_sem=in_send.at[16],
        recv_sem=in_recv.at[16],
        device_id={"core": other},
        device_id_type=MESH_ID,
    )

    barrier = pltpu.get_barrier_semaphore()
    neighbours = [{"core": other}]
    for place, n, me in ((at_x, 4, x), (at_y, 4, y), (at_z, 8, z)):
        neighbours += [step_on(place, n, me)(0), step_on(place, n, me)(1)]
    for device in neighbours:
        pl.semaphore_signal(barrier, inc=1, device_id=device, device_id_type=MESH_ID)
    grads_load.start()
    for block, count in groups:
        for i in range(count):
            own_load(block(i)).start()
    pl.semaphore_wait(barrier, len(neighbours))
    grads_send.start()
    for block, count in groups:
        for i in range(count):
            partner_send(block(i)).start()

    sems = Sems(send_sem, recv_sem)

    def part(ref, width):
        return lambda lead, start, length: ref.at[lead, pl.ds(start, length)]

    x1 = Ring(4, x, step_on(at_x, 4, x), lambda d, h: px.at[d, pl.ds(16 * h, 16)], 16, lx1, sems)
    y1 = Ring(4, y, step_on(at_y, 4, y), lambda d, h: py.at[d, pl.ds(16 * h, 16)], 16, ly1, sems)
    z1 = Ring(8, z, step_on(at_z, 8, z), lambda d, h: pz.at[d, pl.ds(8 * h, 8)], 8, lz1, sems)
    x2 = Ring(4, y, step_on(at_y, 4, y), lambda d, h: px.at[x, pl.ds(8 * d + 4 * h, 4)], 4, lx2, sems)
    y2 = Ring(4, x, step_on(at_x, 4, x), lambda d, h: py.at[y, pl.ds(8 * d + 4 * h, 4)], 4, ly2, sems)
    z2 = Ring(4, y, step_on(at_y, 4, y), lambda d, h: pz.at[z, pl.ds(4 * d + 2 * h, 2)], 2, lz2, sems)
    x3 = Direct(8, z, at_z, lambda d: px.at[x, 8 * y + d], lx3, sems)
    y3 = Direct(8, z, at_z, lambda d: py.at[y, 8 * x + d], ly3, sems)
    z3 = Direct(4, x, at_x, lambda d: pz.at[z, 4 * y + d], lz3, sems)

    grads_load.wait()
    grads_send.wait_recv()

    def product(j):
        own_load(j).wait()
        partner_send(j).wait_recv()
        zl, xj = j // 4, lax.rem(j, 4)
        total = lax.dot_general(
            lhs[j], rhs[...], (((0,), (0,)), ((), ())), preferred_element_type=F32
        ).astype(BF16)
        for yi in range(4):
            for zh in range(2):
                rows = total[(yi * 2 + zh) * ROWS : (yi * 2 + zh + 1) * ROWS]
                zi = zh * 4 + zl
                px[xj, yi * 8 + zi] = rows[:, :CX]
                py[yi, xj * 8 + zi] = rows[:, CX : CX + CY]
                pz[zi, yi * 4 + xj] = rows[:, CX + CY :]

    def products(block, count):
        def body(i, _):
            product(block(i))
            return 0

        lax.fori_loop(0, count, body, 0)

    products(block_a, 4)
    x1.first()
    products(block_b, 3)
    z1.first()
    products(block_c, 9)
    y1.first()
    x1.direct()
    z1.direct()
    y1.direct()
    z1.onward(True, 3)
    x1.onward(True, 1)
    z1.onward(False, 2)
    y1.onward(True, 1)
    z1.onward(True, 2)
    z1.onward(False, 1)
    x1.last()
    x2.first()
    x2.direct()
    y1.last()
    y2.first()
    y2.direct()
    z1.onward(True, 1)
    x2.onward(True, 1)
    y2.onward(True, 1)
    z1.last()
    z2.first()
    z2.direct()
    x2.last()
    x3.start()
    y2.last()
    y3.start()
    z2.onward(True, 1)
    z2.last()
    z3.start()

    def collect(own, landing, count, lanes):
        total = own[...].astype(F32)
        for i in range(count):
            total = total + landing[i].astype(F32)
        out[:, lanes] = total

    x3.arrive()
    collect(px.at[x, 8 * y + z], lx3, 7, pl.ds(0, CX))
    y3.arrive()
    collect(py.at[y, 8 * x + z], ly3, 7, pl.ds(CX, CY))
    z3.arrive()
    collect(pz.at[z, 4 * y + x], lz3, 3, pl.ds(CX + CY, CZ))

    grad = out[...]
    partial = jnp.zeros((8, 128), F32)
    for r in range(0, ROWS, 8):
        for c in range(0, CX + CY + CZ, 128):
            tile = grad[r : r + 8, c : c + 128]
            partial = partial + tile * tile
    square[0] = partial

    def fold(stage, n, me, place, landing):
        exchange = Direct(n, me, place, lambda d: square.at[stage], landing, sems)
        exchange.start()
        exchange.arrive()
        total = square[stage]
        for i in range(n - 1):
            total = total + landing[i]
        square[stage + 1] = total

    fold(0, 8, z, at_z, sqz)
    fold(1, 4, y, at_y, sqy)
    fold(2, 4, x, at_x, sqx)
    fold(3, 2, core, lambda i: {"core": i}, sqc)
    squares = jnp.sum(square[4], keepdims=True)
    limit = jnp.sqrt(jnp.full((1, 1), 8192.0 * 1024.0, F32))
    clip = jnp.minimum(1.0, limit / (jnp.sqrt(squares) + 1e-06))
    out[...] = out[...] * clip

    for copy in sems.sent:
        copy.wait_send()
    grads_send.wait_send()
    for j in range(16):
        partner_send(j).wait_send()


def scaled_gradient(normed, out_grads):
    def landing(n, length, width):
        return pltpu.VMEM((2, n - 1, length, ROWS, width), BF16)

    def pieces(n, width):
        return pltpu.VMEM((n - 1, ROWS, width), BF16)

    n_sems = 6 + 6 + 14 + 6 + 6 + 6 + 7 + 7 + 3 + 7 + 3 + 3 + 1
    return pl.pallas_call(
        kernel,
        out_shape=jax.ShapeDtypeStruct((ROWS, CX + CY + CZ), F32),
        in_specs=[pl.BlockSpec(memory_space=pl.ANY)] * 2,
        out_specs=pl.BlockSpec(memory_space=pltpu.VMEM),
        scratch_shapes=[
            pltpu.VMEM((16, 2 * TOK, BLOCK), BF16),
            pltpu.VMEM((2 * TOK, CX + CY + CZ), BF16),
            pltpu.VMEM((4, 32, ROWS, CX), BF16),
            pltpu.VMEM((4, 32, ROWS, CY), BF16),
            pltpu.VMEM((8, 16, ROWS, CZ), BF16),
            landing(4, 16, CX),
            landing(4, 16, CY),
            landing(8, 8, CZ),
            landing(4, 4, CX),
            landing(4, 4, CY),
            landing(4, 2, CZ),
            pieces(8, CX),
            pieces(8, CY),
            pieces(4, CZ),
            pltpu.VMEM((5, 8, 128), F32),
            pltpu.VMEM((7, 8, 128), F32),
            pltpu.VMEM((3, 8, 128), F32),
            pltpu.VMEM((3, 8, 128), F32),
            pltpu.VMEM((1, 8, 128), F32),
            pltpu.SemaphoreType.DMA((n_sems,)),
            pltpu.SemaphoreType.DMA((n_sems,)),
            pltpu.SemaphoreType.DMA((17,)),
            pltpu.SemaphoreType.DMA((17,)),
            pltpu.SemaphoreType.DMA((17,)),
        ],
        compiler_params=pltpu.CompilerParams(collective_id=0, has_side_effects=True),
    )(normed, out_grads)


def shards(normed, out_grads, weight, moment, variance):
    scaled = scaled_gradient(normed, out_grads)
    new_moment = 0.9 * moment + 0.1 * scaled
    new_variance = 0.95 * variance + 0.05 * scaled * scaled
    first = new_moment / (1.0 - 0.9**STEP)
    second = new_variance / (1.0 - 0.95**STEP)
    new_weight = weight - 0.01 * (first / (jnp.sqrt(second) + 1e-08) + 0.1 * weight)
    return (new_weight, new_moment, new_variance)


def solution(mesh):
    split = Mesh(mesh.devices.reshape(SIZES), AXES)
    spec = P(AXES, None)
    return jax.shard_map(
        shards, mesh=split, in_specs=(spec,) * 5, out_specs=(spec,) * 3, check_vma=False
    )
```

time: 329 us -> 78.4 us (0.24)
  waiting for transfers between devices: 163 us -> 0 us
  blocking collectives: 102 us -> 0 us
  Pallas kernels: 0 us -> 75.9 us
  between operations: 14.8 us -> 0.69 us
  starting transfers between devices: 11.7 us -> 0 us
  local copies, waits for them, and re-layouts: 11.7 us -> 0.01 us
  other arithmetic: 13.1 us -> 1.7 us
  matrix products: 10.9 us -> 0 us
    all_gather x1 -> x0, waiting for transfers between devices: 162 us -> none  [shards(): piece = lax.all_gather(out_grads, SHARD, axis=0, tiled=True)]
    pallas_call x0 -> x1, Pallas kernels: none -> 75.9 us  [scaled_gradient(): pl.pallas_call(kernel, out_shape=jax.ShapeDtypeStruct((ROWS, CX + CY + CZ...]
    all_to_all x2 -> x0, blocking collectives: 60.4 us -> none  [the longest x1 51.5 us: sum_in_two_steps(): lax.all_to_all(nearer, far, split_axis=0, concat_axis=0, tiled=True)]
    psum x5 -> x0, blocking collectives: 41.3 us -> none  [by_axis(): return functools.reduce(lax.psum, axes, shard)]
    reduce_sum x4 -> x0, other arithmetic: 12.3 us -> none  [the longest x1 7.2 us: shards(): summed = jnp.sum(to_wire(parts), axis=0)]
    all_to_all x1 -> x0, starting transfers between devices: 11.6 us -> none  [shards(): mine = lax.all_to_all(grid, SHARD, split_axis=2, concat_axis=0, tiled=True)]
    dot_general x1 -> x0, matrix products: 10.9 us -> none  [shards(): jnp.einsum('ktd,ktc->kdc', picked, piece.reshape(count, TOK_DEV, columns)...]
    unnamed x7 -> x6, local copies, waits for them, and re-layouts: 6.4 us -> 0.01 us
  transfers between devices with their start and end apart: 2 -> 0, of which waited for: 1 -> 0; matrix products, arithmetic and copies ran while one was open for 3% -> 0% of each run, Pallas kernels for 0% -> 0%
where the time goes in v1:
time: 78.4 us; the launch traced here: 78.3 us
  Pallas kernels  75.9 us (97%)
  other arithmetic  1.7 us (2%)
    pallas_call x1, Pallas kernels, scaled_gradient(): pl.pallas_call(kernel, out_shape=jax.ShapeDtypeStruct((ROWS, CX + CY + CZ...  75.9 us
    sub x1, other arithmetic, shards(): weight - 0.01 * (first / (jnp.sqrt(second) + 1e-08) + 0.1 * weight)  1.7 us

profile of v1, /device:TPU:1, one launch (start us, length us, event | category | flops | bytes accessed | tf_op | source)
XLA Modules:
  0.0 78.3 jit_solution(3747335116063810455)
XLA Ops:
  0.6 0.0 copy-start.2
  0.6 0.0 copy-start.1
  0.7 0.0 copy-start
  0.7 75.9 %shard_map.76 = f32[32,1024]{1,0:T(8,128)} custom-call(bf16[256,8192]{1,0:T(8,128)(2,1)} %normed.1, bf16[256,1024]{1,0:T(8,128)(2,1)} %out_grads.1), custom_call_target="tpu_custom_call" | custom-call | tf_op jit(solution)/shard_map/pallas_call | solution.py:335
  76.6 0.0 copy-done.2
  76.6 0.0 copy-done.1
  76.6 0.0 copy-done
  76.6 1.7 %multiply_subtract_fusion = (f32[32,1024]{1,0:T(8,128)}, f32[32,1024]{1,0:T(8,128)}, f32[32,1024]{1,0:T(8,128)}) fusion(f32[32,1024]{1,0:T(8,128)S(1)} %copy-done, f32[32,1024]{1,0:T(8,128)} %shard_map.76, f32[32,1024]{1,0:T(8,128)S(1)} %copy-done.1, f32[32,1024]{1,0:T(8,128)S(1)} %copy-done.2), kind=kLoop, calls=%fused_computation.2 | loop fusion | flops 491520 | bytes 917504 | tf_op jit(solution)/shard_map/sub | solution.py:376
Async XLA Ops:
  0.6 76.0 %copy-start.2 = (f32[32,1024]{1,0:T(8,128)S(1)}, f32[32,1024]{1,0:T(8,128)}, u32[]{:S(2)}) copy-start(f32[32,1024]{1,0:T(8,128)} %param.9) | copy-start | bytes 393220
  0.6 76.0 %copy-start.1 = (f32[32,1024]{1,0:T(8,128)S(1)}, f32[32,1024]{1,0:T(8,128)}, u32[]{:S(2)}) copy-start(f32[32,1024]{1,0:T(8,128)} %param.8) | copy-start | bytes 393220
  0.7 76.0 %copy-start = (f32[32,1024]{1,0:T(8,128)S(1)}, f32[32,1024]{1,0:T(8,128)}, u32[]{:S(2)}) copy-start(f32[32,1024]{1,0:T(8,128)} %param.7) | copy-start | bytes 393220

commit v2 on v0

v2 whole, which is shorter than its diff:
```python
import jax
import jax.numpy as jnp
from jax import lax
from jax.experimental import pallas as pl
from jax.experimental.pallas import tpu as pltpu
from jax.sharding import Mesh
from jax.sharding import PartitionSpec as P

STEP = 10
AXES = ("z_lo", "x", "core", "y", "z_hi")
SIZES = (4, 4, 2, 4, 2)
MESH_ID = pl.DeviceIdType.MESH
F32, BF16 = jnp.float32, jnp.bfloat16
D, C, TOK, BLOCK, ROWS = 8192, 1024, 256, 256, 32

STREAMS = ("xyz", "yxz", "zxy")
UNITS = (5, 5, 6)
LENGTH = {"x": 4, "y": 4, "z": 8}
FAR_FIRST = {4: (2, 3, 1, 0), 8: (4, 5, 3, 6, 2, 7, 1, 0)}
PRODUCTS_FIRST, PRODUCTS_NEXT, RATE, LATE, ADDS, SLACK = 6.4, 1.95, 93.6e3, 1.5, 0.9e6, 3.0


def ring_length(s, k):
    return LENGTH[STREAMS[s][k]]


def is_ring(s, k):
    return k < 2 or STREAMS[s][2] == "z"


def piece_count(s, k):
    return (ring_length(s, 1), 2, 1)[k]


def piece_length(s, k):
    return (ring_length(s, 2), ring_length(s, 2) // 2, 1)[k]


def reach(n, way, piece):
    return n // 2 if way == piece % 2 else n // 2 - 1


def hops(s, k):
    for piece in range(piece_count(s, k)):
        for way in (0, 1):
            for hop in range(1, reach(ring_length(s, k), way, piece) + 1):
                yield way, piece, hop


def plan():
    tasks = [("g", i) for i in range(4)]
    for s in range(3):
        for k in range(3):
            if is_ring(s, k):
                tasks += [("l", s, k, piece) for piece in range(piece_count(s, k))]
                tasks += [("s", s, k, *which) for which in hops(s, k)]
            else:
                tasks.append(("d", s))
    link, arrive, done, order = {}, {}, {}, []

    def size(s, k):
        return piece_length(s, k) * UNITS[s] * 16 * 128 * 2

    def own(s, k, piece, off):
        if k == 0:
            first, second = STREAMS[s][:2]
            if first == "x":
                return [("g", FAR_FIRST[4].index(off))]
            return [("g", piece if second == "x" else 3)]
        if k == 1:
            return [("l", s, 0, FAR_FIRST[ring_length(s, 1)].index(off))]
        return [("l", s, 1, 0), ("l", s, 1, 1)]

    def fresh(t):
        return t[0] == "s" and t[5] == reach(ring_length(t[1], t[2]), t[3], t[4])

    def filler(t):
        return fresh(t) and t[5] < ring_length(t[1], t[2]) // 2

    def ready(t):
        if t[0] == "g":
            return 0.0 if t[1] == 0 or ("g", t[1] - 1) in done else None
        came = []
        if t[0] == "d":
            need = own(t[1], 2, 0, 0)
        elif t[0] == "s":
            s, k, way, piece, hop = t[1:]
            n = ring_length(s, k)
            need = own(s, k, piece, hop if way == 0 else n - hop)
            came = [] if fresh(t) else [(s, k, way, piece, hop + 1)]
        else:
            s, k, piece = t[1:]
            need = own(s, k, piece, 0)
            came = [(s, k, way, piece, 1) for way in (0, 1)]
        if any(d not in done for d in need) or any(a not in arrive for a in came):
            return None
        at = max([done[d] for d in need] + [arrive[a] for a in came])
        if filler(t):
            at = max(at, link.get((STREAMS[t[1]][t[2]], t[3]), 0.0) - SLACK)
        return at

    def rank(t):
        if t[0] == "d":
            return (0,)
        if t[0] == "s":
            return (3 if filler(t) else 1, -t[2], -t[5], t[4])
        return (2, -t[2], t[3]) if t[0] == "l" else (4, t[1])

    now = 0.0
    while tasks:
        times = {t: ready(t) for t in tasks}
        able = [t for t in tasks if times[t] is not None and times[t] <= now + 1e-9]
        if not able:
            now = min(v for v in times.values() if v is not None)
            continue
        t = min(able, key=rank)
        tasks.remove(t)
        order.append(t)
        if t[0] == "g":
            now = max(now, PRODUCTS_FIRST) if t[1] == 0 else now + PRODUCTS_NEXT
        elif t[0] == "l":
            now += 3 * size(t[1], t[2]) / 4 / ADDS
        elif t[0] == "s":
            s, k, way, piece, hop = t[1:]
            now += 0.0 if fresh(t) else size(s, k) / 2 / ADDS
            key = (STREAMS[s][k], way)
            link[key] = max(now + 0.05, link.get(key, 0.0)) + 2 * size(s, k) / RATE
            arrive[t[1:]] = link[key] + LATE
        done[t] = now
    return order


class Sems:
    def __init__(self, send, recv):
        self.send, self.recv, self.used, self.sent = send, recv, 0, []

    def start(self, copy):
        copy.start()
        self.sent.append(copy)

    def copy(self, source, target, device):
        self.used += 1
        return pltpu.make_async_remote_copy(
            src_ref=source,
            dst_ref=target,
            send_sem=self.send.at[self.used - 1],
            recv_sem=self.recv.at[self.used - 1],
            device_id=device,
            device_id_type=MESH_ID,
        )


class Ring:
    def __init__(self, s, k, me, place, view, landing, sems):
        self.n, self.me, self.view, self.sems = ring_length(s, k), me, view, sems
        self.length, self.copies, self.came = piece_length(s, k), {}, {}
        used = [0, 0]
        for way, piece, hop in hops(s, k):
            slot = landing.at[way, used[way]]
            used[way] += 1
            self.came[way, piece, hop] = slot
            self.copies[way, piece, hop] = sems.copy(
                view(self.dest(way, hop), piece), slot, place(self.dest(way, 1))
            )

    def dest(self, way, hop):
        return lax.rem(self.me + (hop if way == 0 else self.n - hop), self.n)

    def send(self, way, piece, hop):
        if hop < reach(self.n, way, piece):
            self.copies[way, piece, hop + 1].wait_recv()
            target, came = self.view(self.dest(way, hop), piece), self.came[way, piece, hop + 1]

            def add(i, _):
                target[i] = (target[i].astype(F32) + came[i].astype(F32)).astype(BF16)
                return 0

            lax.fori_loop(0, self.length, add, 0)
        self.sems.start(self.copies[way, piece, hop])

    def arrive(self, piece):
        for way in (0, 1):
            self.copies[way, piece, 1].wait_recv()
        return self.came[0, piece, 1], self.came[1, piece, 1]

    def last(self, piece):
        a, b = self.arrive(piece)
        target = self.view(self.me, piece)

        def add(i, _):
            total = target[i].astype(F32) + a[i].astype(F32)
            target[i] = (total + b[i].astype(F32)).astype(BF16)
            return 0

        lax.fori_loop(0, self.length, add, 0)


def kernel(normed, out_grads, out, lhs, rhs, *refs):
    partials, landings = refs[:3], (refs[3:6], refs[6:9], refs[9:12])
    squares, send_sem, recv_sem, load_sem, in_send, in_recv, heard = refs[12:]
    x, y, core = lax.axis_index("x"), lax.axis_index("y"), lax.axis_index("core")
    z_lo, z_hi = lax.axis_index("z_lo"), lax.axis_index("z_hi")
    place_of = {
        "x": lambda i: {"x": i},
        "y": lambda i: {"y": i},
        "z": lambda i: {"z_hi": i // 4, "z_lo": lax.rem(i, 4)},
    }
    here = {"x": x, "y": y, "z": z_hi * 4 + z_lo}
    other = 1 - core

    def columns(j, c):
        return pl.ds(pl.multiple_of((2 * j + c) * BLOCK, BLOCK), BLOCK)

    def own_load(j):
        return pltpu.make_async_copy(
            normed.at[:, columns(j, core)], lhs.at[j, pl.ds(0, TOK)], load_sem.at[j]
        )

    def partner_copy(source, target, j):
        return pltpu.make_async_remote_copy(
            src_ref=source,
            dst_ref=target,
            send_sem=in_send.at[j],
            recv_sem=in_recv.at[j],
            device_id={"core": other},
            device_id_type=MESH_ID,
        )

    def partner_send(j):
        return partner_copy(normed.at[:, columns(j, other)], lhs.at[j, pl.ds(TOK, TOK)], j)

    blocks = [i * 4 + lax.rem(x + off, 4) for off in FAR_FIRST[4] for i in range(4)]
    grads_load = pltpu.make_async_copy(out_grads, rhs.at[pl.ds(0, TOK)], load_sem.at[16])
    grads_send = partner_copy(out_grads, rhs.at[pl.ds(TOK, TOK)], 16)

    barrier = pltpu.get_barrier_semaphore()
    neighbours = [{"core": other}]
    for axis in "xyz":
        for step in (1, LENGTH[axis] - 1):
            neighbours.append(place_of[axis](lax.rem(here[axis] + step, LENGTH[axis])))
    for device in neighbours:
        pl.semaphore_signal(barrier, inc=1, device_id=device, device_id_type=MESH_ID)
    grads_load.start()
    for j in blocks:
        own_load(j).start()
    pl.semaphore_wait(barrier, len(neighbours))
    grads_send.start()
    for j in blocks:
        partner_send(j).start()

    sems = Sems(send_sem, recv_sem)
    firsts = [sum(UNITS[:s]) for s in range(3)]

    def tile(s, i):
        unit = firsts[s] + i
        return slice(unit // 8 * 16, unit // 8 * 16 + 16), slice(unit % 8 * 128, unit % 8 * 128 + 128)

    def views(s):
        ref = partials[s]
        a1, a2, a3 = STREAMS[s]
        n2, n3 = LENGTH[a2], LENGTH[a3]

        def first(dest, piece):
            i2 = lax.rem(here[a2] + FAR_FIRST[n2][piece], n2)
            return ref.at[dest, pl.ds(n3 * i2, n3)]

        def second(dest, piece):
            return ref.at[here[a1], pl.ds(n3 * dest + n3 // 2 * piece, n3 // 2)]

        def third(dest, piece=0):
            return ref.at[here[a1], pl.ds(n3 * here[a2] + dest, 1)]

        return first, second, third

    stages, directs = {}, {}
    for s in range(3):
        for k in range(3):
            axis, view, landing = STREAMS[s][k], views(s)[k], landings[k][s]
            if is_ring(s, k):
                stages[s, k] = Ring(s, k, here[axis], place_of[axis], view, landing, sems)
            else:
                directs[s] = []
                for off in range(1, LENGTH[axis]):
                    dest = lax.rem(here[axis] + off, LENGTH[axis])
                    directs[s].append(sems.copy(view(dest), landing.at[off - 1], place_of[axis](dest)))

    grads_load.wait()
    grads_send.wait_recv()

    def products(i):
        xj = lax.rem(x + FAR_FIRST[4][i], 4)

        def body(zl, _):
            j = zl * 4 + xj
            own_load(j).wait()
            partner_send(j).wait_recv()
            total = lax.dot_general(
                lhs[j], rhs[...], (((0,), (0,)), ((), ())), preferred_element_type=F32
            ).astype(BF16)
            for yi in range(4):
                for zh in range(2):
                    at = {"x": xj, "y": yi, "z": zh * 4 + zl}
                    rows = total[(yi * 2 + zh) * ROWS : (yi * 2 + zh + 1) * ROWS]
                    for s, (a1, a2, a3) in enumerate(STREAMS):
                        for u in range(UNITS[s]):
                            place = at[a2] * LENGTH[a3] + at[a3]
                            partials[s][at[a1], place, u * 16 : u * 16 + 16] = rows[tile(s, u)]
            return 0

        lax.fori_loop(0, 4, body, 0)

    sums = jnp.zeros((8, 128), F32)

    def finish(s, total, sums):
        for u in range(UNITS[s]):
            part = total[u * 16 : u * 16 + 16]
            out[tile(s, u)] = part
            sums = sums + part[:8] * part[:8] + part[8:] * part[8:]
        return sums

    order = plan()
    rounds = [t for t in order if t[:3] == ("l", 2, 0)]
    for t in order:
        if t[0] == "g":
            products(t[1])
        elif t[0] == "d":
            for copy in directs[t[1]]:
                sems.start(copy)
        elif t[0] == "s":
            stages[t[1], t[2]].send(*t[3:])
        elif t[2] < 2:
            stages[t[1], t[2]].last(t[3])
        else:
            ring = stages[t[1], 2]
            a, b = ring.arrive(0)
            total = ring.view(ring.me, 0)[0].astype(F32) + a[0].astype(F32)
            sums = finish(t[1], total + b[0].astype(F32), sums)
        if t == rounds[-1]:
            pl.semaphore_signal(heard, inc=1, device_id={"core": other}, device_id_type=MESH_ID)
    for s, copies in directs.items():
        total = views(s)[2](here[STREAMS[s][2]])[0].astype(F32)
        for i, copy in enumerate(copies):
            copy.wait_recv()
            total = total + landings[2][s][i, 0].astype(F32)
        sums = finish(s, total, sums)
    pl.semaphore_wait(heard, 1)

    def fold(box, part, offsets, place):
        box[0:1] = part
        copies = []
        for i, off in enumerate(offsets):
            copies.append(sems.copy(box.at[pl.ds(0, 1)], box.at[pl.ds(i + 1, 1)], place(off)))
            sems.start(copies[-1])
        for copy in copies:
            copy.wait_recv()
        return jnp.sum(box[...], axis=0, keepdims=True)

    def along_z(off):
        return {**place_of["z"](lax.rem(here["z"] + off[1], 8)), "core": lax.rem(core + off[0], 2)}

    def across(off):
        return {"x": lax.rem(x + off[0], 4), "y": lax.rem(y + off[1], 4)}

    part = jnp.sum(sums, axis=0, keepdims=True)
    part = fold(squares.at[0], part, [(c, i) for i in FAR_FIRST[8] for c in (1, 0)][:-1], along_z)
    part = fold(squares.at[1], part, [(i, k) for i in FAR_FIRST[4] for k in FAR_FIRST[4]][:-1], across)
    total = jnp.sum(part, axis=1, keepdims=True)
    limit = jnp.sqrt(jnp.full((1, 1), float(D * C), F32))
    clip = jnp.minimum(1.0, limit / (jnp.sqrt(total) + 1e-06))
    out[...] = out[...] * clip

    for copy in sems.sent:
        copy.wait_send()
    grads_send.wait_send()
    for j in range(16):
        partner_send(j).wait_send()


def scaled_gradient(normed, out_grads):
    partials, landings, copies = [], [], 30
    for s in range(3):
        n1, n2, n3 = (ring_length(s, k) for k in range(3))
        partials.append(pltpu.VMEM((n1, n2 * n3, UNITS[s] * 16, 128), BF16))
    for k in range(3):
        for s in range(3):
            tail = (piece_length(s, k), UNITS[s] * 16, 128)
            if is_ring(s, k):
                ways = [way for way, _, _ in hops(s, k)]
                landings.append(pltpu.VMEM((2, max(ways.count(0), ways.count(1)), *tail), BF16))
                copies += len(ways)
            else:
                landings.append(pltpu.VMEM((ring_length(s, k) - 1, *tail), BF16))
                copies += ring_length(s, k) - 1
    return pl.pallas_call(
        kernel,
        out_shape=jax.ShapeDtypeStruct((ROWS, C), F32),
        in_specs=[pl.BlockSpec(memory_space=pl.ANY)] * 2,
        out_specs=pl.BlockSpec(memory_space=pltpu.VMEM),
        scratch_shapes=[
            pltpu.VMEM((16, 2 * TOK, BLOCK), BF16),
            pltpu.VMEM((2 * TOK, C), BF16),
            *partials,
            *landings,
            pltpu.VMEM((2, 16, 128), F32),
            pltpu.SemaphoreType.DMA((copies,)),
            pltpu.SemaphoreType.DMA((copies,)),
            pltpu.SemaphoreType.DMA((17,)),
            pltpu.SemaphoreType.DMA((17,)),
            pltpu.SemaphoreType.DMA((17,)),
            pltpu.SemaphoreType.REGULAR,
        ],
        compiler_params=pltpu.CompilerParams(collective_id=0, has_side_effects=True),
    )(normed, out_grads)


def shards(normed, out_grads, weight, moment, variance):
    scaled = scaled_gradient(normed, out_grads)
    new_moment = 0.9 * moment + 0.1 * scaled
    new_variance = 0.95 * variance + 0.05 * scaled * scaled
    first = new_moment / (1.0 - 0.9**STEP)
    second = new_variance / (1.0 - 0.95**STEP)
    new_weight = weight - 0.01 * (first / (jnp.sqrt(second) + 1e-08) + 0.1 * weight)
    return (new_weight, new_moment, new_variance)


def solution(mesh):
    split = Mesh(mesh.devices.reshape(SIZES), AXES)
    spec = P(AXES, None)
    return jax.shard_map(
        shards, mesh=split, in_specs=(spec,) * 5, out_specs=(spec,) * 3, check_vma=False
    )
```

time: 329 us -> 70.2 us (0.21)
  waiting for transfers between devices: 163 us -> 0 us
  blocking collectives: 102 us -> 0 us
  Pallas kernels: 0 us -> 67.6 us
  between operations: 14.8 us -> 0.69 us
  starting transfers between devices: 11.7 us -> 0 us
  local copies, waits for them, and re-layouts: 11.7 us -> 0.01 us
  other arithmetic: 13.1 us -> 1.7 us
  matrix products: 10.9 us -> 0 us
    all_gather x1 -> x0, waiting for transfers between devices: 162 us -> none  [shards(): piece = lax.all_gather(out_grads, SHARD, axis=0, tiled=True)]
    pallas_call x0 -> x1, Pallas kernels: none -> 67.6 us  [scaled_gradient(): pl.pallas_call(kernel, out_shape=jax.ShapeDtypeStruct((ROWS, C), F32), in...]
    all_to_all x2 -> x0, blocking collectives: 60.4 us -> none  [the longest x1 51.5 us: sum_in_two_steps(): lax.all_to_all(nearer, far, split_axis=0, concat_axis=0, tiled=True)]
    psum x5 -> x0, blocking collectives: 41.3 us -> none  [by_axis(): return functools.reduce(lax.psum, axes, shard)]
    reduce_sum x4 -> x0, other arithmetic: 12.3 us -> none  [the longest x1 7.2 us: shards(): summed = jnp.sum(to_wire(parts), axis=0)]
    all_to_all x1 -> x0, starting transfers between devices: 11.6 us -> none  [shards(): mine = lax.all_to_all(grid, SHARD, split_axis=2, concat_axis=0, tiled=True)]
    dot_general x1 -> x0, matrix products: 10.9 us -> none  [shards(): jnp.einsum('ktd,ktc->kdc', picked, piece.reshape(count, TOK_DEV, columns)...]
    unnamed x7 -> x6, local copies, waits for them, and re-layouts: 6.4 us -> 0.01 us
  transfers between devices with their start and end apart: 2 -> 0, of which waited for: 1 -> 0; matrix products, arithmetic and copies ran while one was open for 3% -> 0% of each run, Pallas kernels for 0% -> 0%
where the time goes in v2:
time: 70.2 us; the launch traced here: 70 us
  Pallas kernels  67.6 us (96%)
  other arithmetic  1.7 us (2%)
    pallas_call x1, Pallas kernels, scaled_gradient(): pl.pallas_call(kernel, out_shape=jax.ShapeDtypeStruct((ROWS, C), F32), in...  67.6 us
    sub x1, other arithmetic, shards(): weight - 0.01 * (first / (jnp.sqrt(second) + 1e-08) + 0.1 * weight)  1.7 us

profile of v2, /device:TPU:1, one launch (start us, length us, event | category | flops | bytes accessed | tf_op | source)
XLA Modules:
  0.0 70.0 jit_solution(1949033095405233320)
XLA Ops:
  0.6 0.0 copy-start.2
  0.6 0.0 copy-start.1
  0.7 0.0 copy-start
  0.7 67.6 %shard_map.76 = f32[32,1024]{1,0:T(8,128)} custom-call(bf16[256,8192]{1,0:T(8,128)(2,1)} %normed.1, bf16[256,1024]{1,0:T(8,128)(2,1)} %out_grads.1), custom_call_target="tpu_custom_call" | custom-call | tf_op jit(solution)/shard_map/pallas_call | solution.py:394
  68.3 0.0 copy-done.2
  68.3 0.0 copy-done.1
  68.3 0.0 copy-done
  68.3 1.7 %multiply_subtract_fusion = (f32[32,1024]{1,0:T(8,128)}, f32[32,1024]{1,0:T(8,128)}, f32[32,1024]{1,0:T(8,128)}) fusion(f32[32,1024]{1,0:T(8,128)S(1)} %copy-done, f32[32,1024]{1,0:T(8,128)} %shard_map.76, f32[32,1024]{1,0:T(8,128)S(1)} %copy-done.1, f32[32,1024]{1,0:T(8,128)S(1)} %copy-done.2), kind=kLoop, calls=%fused_computation.2 | loop fusion | flops 491520 | bytes 917504 | tf_op jit(solution)/shard_map/sub | solution.py:422
Async XLA Ops:
  0.6 67.7 %copy-start.2 = (f32[32,1024]{1,0:T(8,128)S(1)}, f32[32,1024]{1,0:T(8,128)}, u32[]{:S(2)}) copy-start(f32[32,1024]{1,0:T(8,128)} %param.9) | copy-start | bytes 393220
  0.6 67.7 %copy-start.1 = (f32[32,1024]{1,0:T(8,128)S(1)}, f32[32,1024]{1,0:T(8,128)}, u32[]{:S(2)}) copy-start(f32[32,1024]{1,0:T(8,128)} %param.8) | copy-start | bytes 393220
  0.7 67.7 %copy-start = (f32[32,1024]{1,0:T(8,128)S(1)}, f32[32,1024]{1,0:T(8,128)}, u32[]{:S(2)}) copy-start(f32[32,1024]{1,0:T(8,128)} %param.7) | copy-start | bytes 393220

commit v3 on v2

v3 whole, which is shorter than its diff:
```python
import jax
import jax.numpy as jnp
from jax import lax
from jax.experimental import pallas as pl
from jax.experimental.pallas import tpu as pltpu
from jax.sharding import Mesh
from jax.sharding import PartitionSpec as P

STEP = 10
AXES = ("z_lo", "x", "core", "y", "z_hi")
SIZES = (4, 4, 2, 4, 2)
MESH_ID = pl.DeviceIdType.MESH
F32, BF16 = jnp.float32, jnp.bfloat16
D, C, TOK, BLOCK, ROWS = 8192, 1024, 256, 256, 32

STREAMS = ("xzy", "yzx", "zxy")
UNITS = (6, 6, 4)
LENGTH = {"x": 4, "y": 4, "z": 8}
FAR_FIRST = {4: (2, 3, 1, 0), 8: (4, 5, 3, 6, 2, 7, 1, 0)}
GROUPS = (4, 3, 3, 3, 3)
LATER = {1: 2, 3: 3, 2: 4}
PRODUCTS_FIRST, PRODUCTS_NEXT, RATE, LATE, ADDS, SLACK = 6.4, 1.45, 93.6e3, 2.0, 0.9e6, 3.0


def ring_length(s, k):
    return LENGTH[STREAMS[s][k]]


def is_ring(s, k):
    return k < 2 or STREAMS[s][2] == "z"


def piece_count(s, k):
    return (ring_length(s, 1), 2, 1)[k]


def piece_length(s, k):
    return (ring_length(s, 2), ring_length(s, 2) // 2, 1)[k]


def reach(n, way, piece):
    return n // 2 if way == piece % 2 else n // 2 - 1


def hops(s, k):
    for piece in range(piece_count(s, k)):
        for way in (0, 1):
            for hop in range(1, reach(ring_length(s, k), way, piece) + 1):
                yield way, piece, hop


def plan():
    tasks = [("g", i) for i in range(5)]
    for s in range(len(STREAMS)):
        for k in range(3):
            if is_ring(s, k):
                tasks += [("l", s, k, piece) for piece in range(piece_count(s, k))]
                tasks += [("s", s, k, *which) for which in hops(s, k)]
            else:
                tasks.append(("d", s))
    link, arrive, done, order = {}, {}, {}, []

    def size(s, k):
        return piece_length(s, k) * UNITS[s] * 16 * 128 * 2

    def own(s, k, piece, off):
        if k == 0:
            at = {STREAMS[s][0]: off, STREAMS[s][1]: FAR_FIRST[ring_length(s, 1)][piece]}
            z_lo = at.get("z", 2) % 4
            return [("g", 0 if z_lo == 0 else 1 if at.get("x") == 2 else LATER[z_lo])]
        if k == 1:
            return [("l", s, 0, FAR_FIRST[ring_length(s, 1)].index(off))]
        return [("l", s, 1, 0), ("l", s, 1, 1)]

    def fresh(t):
        return t[0] == "s" and t[5] == reach(ring_length(t[1], t[2]), t[3], t[4])

    def filler(t):
        return fresh(t) and t[5] < ring_length(t[1], t[2]) // 2

    def ready(t):
        if t[0] == "g":
            return 0.0 if t[1] == 0 or ("g", t[1] - 1) in done else None
        came = []
        if t[0] == "d":
            need = own(t[1], 2, 0, 0)
        elif t[0] == "s":
            s, k, way, piece, hop = t[1:]
            n = ring_length(s, k)
            need = own(s, k, piece, hop if way == 0 else n - hop)
            came = [] if fresh(t) else [(s, k, way, piece, hop + 1)]
        else:
            s, k, piece = t[1:]
            need = own(s, k, piece, 0)
            came = [(s, k, way, piece, 1) for way in (0, 1)]
        if any(d not in done for d in need) or any(a not in arrive for a in came):
            return None
        at = max([done[d] for d in need] + [arrive[a] for a in came])
        if filler(t):
            at = max(at, link.get((STREAMS[t[1]][t[2]], t[3]), 0.0) - SLACK)
        return at

    def rank(t):
        if t[0] == "d":
            return (0,)
        if t[0] == "s":
            return (3 if filler(t) else 1, -t[2], -t[5], t[4])
        return (2, -t[2], t[3]) if t[0] == "l" else (4, t[1])

    now = 0.0
    while tasks:
        times = {t: ready(t) for t in tasks}
        able = [t for t in tasks if times[t] is not None and times[t] <= now + 1e-9]
        if not able:
            now = min(v for v in times.values() if v is not None)
            continue
        t = min(able, key=rank)
        tasks.remove(t)
        order.append(t)
        if t[0] == "g":
            now = max(now, PRODUCTS_FIRST) if t[1] == 0 else now + PRODUCTS_NEXT
        elif t[0] == "l":
            now += 3 * size(t[1], t[2]) / 4 / ADDS
        elif t[0] == "s":
            s, k, way, piece, hop = t[1:]
            now += 0.0 if fresh(t) else size(s, k) / 2 / ADDS
            key = (STREAMS[s][k], way)
            link[key] = max(now + 0.05, link.get(key, 0.0)) + 2 * size(s, k) / RATE
            arrive[t[1:]] = link[key] + LATE
        done[t] = now
    return order


def wait(ref, sem):
    pltpu.make_async_copy(ref, ref, sem).wait()


def remote(source, target, send_sem, recv_sem, device):
    return pltpu.make_async_remote_copy(
        src_ref=source,
        dst_ref=target,
        send_sem=send_sem,
        recv_sem=recv_sem,
        device_id=device,
        device_id_type=MESH_ID,
    )


class Sems:
    def __init__(self, ref):
        self.ref, self.used = ref, 0

    def take(self):
        self.used += 1
        return self.ref.at[self.used - 1]


class Ring:
    def __init__(self, s, k, me, place, view, landing, send_sem, sems):
        self.n, self.me, self.view, self.landing = ring_length(s, k), me, view, landing
        self.length, self.copies, self.came = piece_length(s, k), {}, {}
        self.near = [sems.take() for _ in range(piece_count(s, k))]
        slots = 2 * len(self.near)
        for way, piece, hop in hops(s, k):
            if hop == 1:
                slot, sem = 2 * piece + way, self.near[piece]
            else:
                slot, sem = slots, sems.take()
                slots += 1
            self.came[way, piece, hop] = landing.at[slot]
            self.copies[way, piece, hop] = remote(
                view(self.dest(way, hop), piece), landing.at[slot], send_sem, sem, place(self.dest(way, 1))
            )

    def dest(self, way, hop):
        return lax.rem(self.me + (hop if way == 0 else self.n - hop), self.n)

    def send(self, way, piece, hop):
        if hop < reach(self.n, way, piece):
            self.copies[way, piece, hop + 1].wait_recv()
            target, came = self.view(self.dest(way, hop), piece), self.came[way, piece, hop + 1]

            def add(i, _):
                target[i] = (target[i].astype(F32) + came[i].astype(F32)).astype(BF16)
                return 0

            lax.fori_loop(0, self.length, add, 0)
        self.copies[way, piece, hop].start()

    def arrive(self, piece):
        wait(self.landing.at[pl.ds(2 * piece, 2)], self.near[piece])
        return self.came[0, piece, 1], self.came[1, piece, 1]

    def last(self, piece):
        a, b = self.arrive(piece)
        target = self.view(self.me, piece)

        def add(i, _):
            total = target[i].astype(F32) + a[i].astype(F32)
            target[i] = (total + b[i].astype(F32)).astype(BF16)
            return 0

        lax.fori_loop(0, self.length, add, 0)


def kernel(normed, out_grads, out, lhs, rhs, *refs):
    many = len(STREAMS)
    partials = refs[:many]
    landings = [refs[many * (k + 1) : many * (k + 2)] for k in range(3)]
    squares, send_sem, recv_sem, load_sem, in_send, in_recv, fold_sem, heard = refs[many * 4 :]
    x, y, core = lax.axis_index("x"), lax.axis_index("y"), lax.axis_index("core")
    z_lo, z_hi = lax.axis_index("z_lo"), lax.axis_index("z_hi")
    place_of = {
        "x": lambda i: {"x": i},
        "y": lambda i: {"y": i},
        "z": lambda i: {"z_hi": i // 4, "z_lo": lax.rem(i, 4)},
    }
    here = {"x": x, "y": y, "z": z_hi * 4 + z_lo}
    other = 1 - core

    def columns(j, c):
        return pl.ds(pl.multiple_of((2 * j + c) * BLOCK, BLOCK), BLOCK)

    def block(group, i):
        if group == 0:
            return z_lo, lax.rem(x + 2 + i, 4)
        if group == 1:
            return lax.rem(z_lo + 1 + i, 4), lax.rem(x + 2, 4)
        off = next(o for o, g in LATER.items() if g == group)
        return lax.rem(z_lo + off, 4), lax.rem(x + 3 + i, 4)

    before = [sum(GROUPS[:group]) for group in range(len(GROUPS))]

    def own_load(group, i):
        zl, xj = block(group, i)
        return pltpu.make_async_copy(
            normed.at[:, columns(zl * 4 + xj, core)], lhs.at[before[group] + i, pl.ds(0, TOK)], load_sem.at[group]
        )

    def partner_send(group, i):
        zl, xj = block(group, i)
        return remote(
            normed.at[:, columns(zl * 4 + xj, other)],
            lhs.at[before[group] + i, pl.ds(TOK, TOK)],
            in_send.at[0],
            in_recv.at[before[group] + i],
            {"core": other},
        )

    blocks = [(group, i) for group, count in enumerate(GROUPS) for i in range(count)]
    grads_load = pltpu.make_async_copy(out_grads, rhs.at[pl.ds(0, TOK)], load_sem.at[len(GROUPS)])
    grads_send = remote(out_grads, rhs.at[pl.ds(TOK, TOK)], in_send.at[1], in_recv.at[16], {"core": other})

    barrier = pltpu.get_barrier_semaphore()
    neighbours = [{"core": other}]
    for axis in "xyz":
        for step in (1, LENGTH[axis] - 1):
            neighbours.append(place_of[axis](lax.rem(here[axis] + step, LENGTH[axis])))
    for device in neighbours:
        pl.semaphore_signal(barrier, inc=1, device_id=device, device_id_type=MESH_ID)
    grads_load.start()
    for where in blocks:
        own_load(*where).start()
    pl.semaphore_wait(barrier, len(neighbours))
    grads_send.start()
    for where in blocks:
        partner_send(*where).start()

    sems = Sems(recv_sem)
    firsts = [sum(UNITS[:s]) for s in range(len(STREAMS))]

    def tile(s, i):
        unit = firsts[s] + i
        return slice(unit // 8 * 16, unit // 8 * 16 + 16), slice(unit % 8 * 128, unit % 8 * 128 + 128)

    def views(s):
        ref = partials[s]
        a1, a2, a3 = STREAMS[s]
        n2, n3 = LENGTH[a2], LENGTH[a3]
        mine = here[a1] * n2 * n3

        def first(dest, piece):
            i2 = lax.rem(here[a2] + FAR_FIRST[n2][piece], n2)
            return ref.at[pl.ds(dest * n2 * n3 + n3 * i2, n3)]

        def second(dest, piece):
            return ref.at[pl.ds(mine + n3 * dest + n3 // 2 * piece, n3 // 2)]

        def third(dest, piece=0):
            return ref.at[pl.ds(mine + n3 * here[a2] + dest, 1)]

        return first, second, third

    stages, directs = {}, {}
    for s in range(len(STREAMS)):
        for k in range(3):
            axis, view, landing = STREAMS[s][k], views(s)[k], landings[k][s]
            if is_ring(s, k):
                stages[s, k] = Ring(s, k, here[axis], place_of[axis], view, landing, send_sem.at[s], sems)
            else:
                directs[s] = sems.take()

    grads_load.wait()
    grads_send.wait_recv()

    def products(group):
        first = before[group]
        wait(lhs.at[pl.ds(first, GROUPS[group]), pl.ds(0, TOK)], load_sem.at[group])

        def body(i, _):
            partner_send(group, i).wait_recv()
            zl, xj = block(group, i)
            total = lax.dot_general(
                lhs[first + i], rhs[...], (((0,), (0,)), ((), ())), preferred_element_type=F32
            ).astype(BF16)
            for yi in range(4):
                for zh in range(2):
                    at = {"x": xj, "y": yi, "z": zh * 4 + zl}
                    rows = total[(yi * 2 + zh) * ROWS : (yi * 2 + zh + 1) * ROWS]
                    for s, (a1, a2, a3) in enumerate(STREAMS):
                        for u in range(UNITS[s]):
                            place = (at[a1] * LENGTH[a2] + at[a2]) * LENGTH[a3] + at[a3]
                            partials[s][place, u * 16 : u * 16 + 16] = rows[tile(s, u)]
            return 0

        lax.fori_loop(0, GROUPS[group], body, 0)

    sums = jnp.zeros((8, 128), F32)

    def finish(s, total, sums):
        for u in range(UNITS[s]):
            part = total[u * 16 : u * 16 + 16]
            out[tile(s, u)] = part
            sums = sums + part[:8] * part[:8] + part[8:] * part[8:]
        return sums

    order = plan()
    rounds = [t for t in order if t[0] == "l" and t[2] == 0 and STREAMS[t[1]][0] == "z"]
    for t in order:
        if t[0] == "g":
            products(t[1])
        elif t[0] == "d":
            s, axis = t[1], STREAMS[t[1]][2]
            for off in FAR_FIRST[LENGTH[axis]][:-1]:
                dest = lax.rem(here[axis] + off, LENGTH[axis])
                landing = landings[2][s].at[off - 1]
                remote(views(s)[2](dest), landing, send_sem.at[s], directs[s], place_of[axis](dest)).start()
        elif t[0] == "s":
            stages[t[1], t[2]].send(*t[3:])
        elif t[2] < 2:
            stages[t[1], t[2]].last(t[3])
        else:
            ring = stages[t[1], 2]
            a, b = ring.arrive(0)
            total = ring.view(ring.me, 0)[0].astype(F32) + a[0].astype(F32)
            sums = finish(t[1], total + b[0].astype(F32), sums)
        if t == rounds[-1]:
            pl.semaphore_signal(heard, inc=1, device_id={"core": other}, device_id_type=MESH_ID)
    for s, sem in directs.items():
        wait(landings[2][s], sem)
        total = views(s)[2](here[STREAMS[s][2]])[0].astype(F32)
        for i in range(LENGTH[STREAMS[s][2]] - 1):
            total = total + landings[2][s][i, 0].astype(F32)
        sums = finish(s, total, sums)
    pl.semaphore_wait(heard, 1)

    def fold(turn, part, offsets, place):
        box = squares.at[turn]
        box[0:1] = part
        for i, off in enumerate(offsets):
            target = box.at[pl.ds(i + 1, 1)]
            remote(box.at[pl.ds(0, 1)], target, fold_sem.at[turn, 0], fold_sem.at[turn, 1], place(off)).start()
        wait(box.at[pl.ds(1, len(offsets))], fold_sem.at[turn, 1])
        return jnp.sum(box[...], axis=0, keepdims=True)

    def along_z(off):
        return {**place_of["z"](lax.rem(here["z"] + off[1], 8)), "core": lax.rem(core + off[0], 2)}

    def across(off):
        return {"x": lax.rem(x + off[0], 4), "y": lax.rem(y + off[1], 4)}

    part = jnp.sum(sums, axis=0, keepdims=True)
    part = fold(0, part, [(c, i) for i in FAR_FIRST[8] for c in (1, 0)][:-1], along_z)
    part = fold(1, part, [(i, k) for i in FAR_FIRST[4] for k in FAR_FIRST[4]][:-1], across)
    total = jnp.sum(part, axis=1, keepdims=True)
    limit = jnp.sqrt(jnp.full((1, 1), float(D * C), F32))
    clip = jnp.minimum(1.0, limit / (jnp.sqrt(total) + 1e-06))
    out[...] = out[...] * clip

    for s, partial in enumerate(partials):
        wait(partial.at[pl.ds(0, 127)], send_sem.at[s])
    for turn in (0, 1):
        wait(squares.at[turn, pl.ds(1, 15)], fold_sem.at[turn, 0])
    wait(lhs.at[:, pl.ds(0, TOK)], in_send.at[0])
    wait(rhs.at[pl.ds(0, TOK)], in_send.at[1])


def scaled_gradient(normed, out_grads):
    landings, sems, many = [], 0, len(STREAMS)
    partials = [pltpu.VMEM((128, units * 16, 128), BF16) for units in UNITS]
    for k in range(3):
        for s in range(many):
            tail = (piece_length(s, k), UNITS[s] * 16, 128)
            if is_ring(s, k):
                slots = len(list(hops(s, k)))
                sems += slots - piece_count(s, k)
            else:
                slots = ring_length(s, k) - 1
                sems += 1
            landings.append(pltpu.VMEM((slots, *tail), BF16))
    return pl.pallas_call(
        kernel,
        out_shape=pltpu.VMEM((ROWS, C), F32),
        in_specs=[pl.BlockSpec(memory_space=pl.ANY)] * 2,
        out_specs=pl.BlockSpec(memory_space=pltpu.VMEM),
        scratch_shapes=[
            pltpu.VMEM((16, 2 * TOK, BLOCK), BF16),
            pltpu.VMEM((2 * TOK, C), BF16),
            *partials,
            *landings,
            pltpu.VMEM((2, 16, 128), F32),
            pltpu.SemaphoreType.DMA((many,)),
            pltpu.SemaphoreType.DMA((sems,)),
            pltpu.SemaphoreType.DMA((len(GROUPS) + 1,)),
            pltpu.SemaphoreType.DMA((2,)),
            pltpu.SemaphoreType.DMA((17,)),
            pltpu.SemaphoreType.DMA((2, 2)),
            pltpu.SemaphoreType.REGULAR,
        ],
        compiler_params=pltpu.CompilerParams(collective_id=0, has_side_effects=True),
    )(normed, out_grads)


def shards(normed, out_grads, weight, moment, variance):
    scaled = scaled_gradient(normed, out_grads)
    new_moment = 0.9 * moment + 0.1 * scaled
    new_variance = 0.95 * variance + 0.05 * scaled * scaled
    first = new_moment / (1.0 - 0.9**STEP)
    second = new_variance / (1.0 - 0.95**STEP)
    new_weight = weight - 0.01 * (first / (jnp.sqrt(second) + 1e-08) + 0.1 * weight)
    return (new_weight, new_moment, new_variance)


def solution(mesh):
    split = Mesh(mesh.devices.reshape(SIZES), AXES)
    spec = P(AXES, None)
    return jax.shard_map(
        shards, mesh=split, in_specs=(spec,) * 5, out_specs=(spec,) * 3, check_vma=False
    )
```

time: 70.2 us -> 66 us (0.940)
  Pallas kernels: 67.6 us -> 64.4 us
  other arithmetic: 1.7 us -> 0.8 us
    pallas_call x1, Pallas kernels: 67.6 us -> 64.4 us  [scaled_gradient(): pl.pallas_call(kernel, out_shape=pltpu.VMEM((ROWS, C), F32), in_specs=[pl...]
    sub x1, other arithmetic: 1.7 us -> 0.8 us  [shards(): weight - 0.01 * (first / (jnp.sqrt(second) + 1e-08) + 0.1 * weight)]
where the time goes in v3:
time: 66 us; the launch traced here: 65.9 us
  Pallas kernels  64.4 us (98%)
  other arithmetic  0.8 us (1%)
  between operations  0.69 us (1%)
    pallas_call x1, Pallas kernels, scaled_gradient(): pl.pallas_call(kernel, out_shape=pltpu.VMEM((ROWS, C), F32), in_specs=[pl...  64.4 us

profile of v3, /device:TPU:1, one launch (start us, length us, event | category | flops | bytes accessed | tf_op | source)
XLA Modules:
  0.0 65.9 jit_solution(11802391490379479239)
XLA Ops:
  0.6 0.0 copy-start.2
  0.6 0.0 copy-start.1
  0.7 0.0 copy-start
  0.7 64.4 %shard_map.76 = f32[32,1024]{1,0:T(8,128)S(1)} custom-call(bf16[256,8192]{1,0:T(8,128)(2,1)} %normed.1, bf16[256,1024]{1,0:T(8,128)(2,1)} %out_grads.1), custom_call_target="tpu_custom_call" | custom-call | tf_op jit(solution)/shard_map/pallas_call | solution.py:411
  65.1 0.0 copy-done.2
  65.1 0.0 copy-done.1
  65.1 0.0 copy-done
  65.1 0.8 %multiply_subtract_fusion = (f32[32,1024]{1,0:T(8,128)}, f32[32,1024]{1,0:T(8,128)}, f32[32,1024]{1,0:T(8,128)}) fusion(f32[32,1024]{1,0:T(8,128)S(1)} %copy-done, f32[32,1024]{1,0:T(8,128)S(1)} %shard_map.76, f32[32,1024]{1,0:T(8,128)S(1)} %copy-done.1, f32[32,1024]{1,0:T(8,128)S(1)} %copy-done.2), kind=kLoop, calls=%fused_computation.2 | loop fusion | flops 491520 | bytes 917504 | tf_op jit(solution)/shard_map/sub | solution.py:440
Async XLA Ops:
  0.6 64.5 %copy-start.2 = (f32[32,1024]{1,0:T(8,128)S(1)}, f32[32,1024]{1,0:T(8,128)}, u32[]{:S(2)}) copy-start(f32[32,1024]{1,0:T(8,128)} %param.9) | copy-start | bytes 393220
  0.6 64.5 %copy-start.1 = (f32[32,1024]{1,0:T(8,128)S(1)}, f32[32,1024]{1,0:T(8,128)}, u32[]{:S(2)}) copy-start(f32[32,1024]{1,0:T(8,128)} %param.8) | copy-start | bytes 393220
  0.7 64.5 %copy-start = (f32[32,1024]{1,0:T(8,128)S(1)}, f32[32,1024]{1,0:T(8,128)}, u32[]{:S(2)}) copy-start(f32[32,1024]{1,0:T(8,128)} %param.7) | copy-start | bytes 393220

commit v4 on v3

--- a/solution.py
+++ b/solution.py
@@ -17,9 +17,11 @@
 UNITS = (6, 6, 4)
 LENGTH = {"x": 4, "y": 4, "z": 8}
 FAR_FIRST = {4: (2, 3, 1, 0), 8: (4, 5, 3, 6, 2, 7, 1, 0)}
-GROUPS = (4, 3, 3, 3, 3)
-LATER = {1: 2, 3: 3, 2: 4}
-PRODUCTS_FIRST, PRODUCTS_NEXT, RATE, LATE, ADDS, SLACK = 6.4, 1.45, 93.6e3, 2.0, 0.9e6, 3.0
+BLOCKS = (
+    *((0, 2), (0, 3), (0, 1), (0, 0), (1, 2), (3, 3), (1, 1), (3, 0)),
+    *((3, 2), (3, 1), (1, 3), (1, 0), (2, 2), (2, 3), (2, 1), (2, 0)),
+)
+PRODUCTS_FIRST, PRODUCTS_NEXT, RATE, LATE, ADDS, SLACK = 5.1, 0.47, 93.6e3, 2.0, 0.9e6, 3.0
 
 
 def ring_length(s, k):
@@ -50,7 +52,7 @@
 
 
 def plan():
-    tasks = [("g", i) for i in range(5)]
+    tasks = [("g", i) for i in range(16)]
     for s in range(len(STREAMS)):
         for k in range(3):
             if is_ring(s, k):
@@ -66,8 +68,9 @@
     def own(s, k, piece, off):
         if k == 0:
             at = {STREAMS[s][0]: off, STREAMS[s][1]: FAR_FIRST[ring_length(s, 1)][piece]}
-            z_lo = at.get("z", 2) % 4
-            return [("g", 0 if z_lo == 0 else 1 if at.get("x") == 2 else LATER[z_lo])]
+            z_los = [at["z"] % 4] if "z" in at else range(4)
+            xs = [at["x"]] if "x" in at else range(4)
+            return [("g", max(BLOCKS.index((z_lo, x)) for z_lo in z_los for x in xs))]
         if k == 1:
             return [("l", s, 0, FAR_FIRST[ring_length(s, 1)].index(off))]
         return [("l", s, 1, 0), ("l", s, 1, 1)]
@@ -221,34 +224,26 @@
     def columns(j, c):
         return pl.ds(pl.multiple_of((2 * j + c) * BLOCK, BLOCK), BLOCK)
 
-    def block(group, i):
-        if group == 0:
-            return z_lo, lax.rem(x + 2 + i, 4)
-        if group == 1:
-            return lax.rem(z_lo + 1 + i, 4), lax.rem(x + 2, 4)
-        off = next(o for o, g in LATER.items() if g == group)
-        return lax.rem(z_lo + off, 4), lax.rem(x + 3 + i, 4)
-
-    before = [sum(GROUPS[:group]) for group in range(len(GROUPS))]
-
-    def own_load(group, i):
-        zl, xj = block(group, i)
+    def block(pos):
+        return lax.rem(z_lo + BLOCKS[pos][0], 4), lax.rem(x + BLOCKS[pos][1], 4)
+
+    def own_load(pos):
+        zl, xj = block(pos)
         return pltpu.make_async_copy(
-            normed.at[:, columns(zl * 4 + xj, core)], lhs.at[before[group] + i, pl.ds(0, TOK)], load_sem.at[group]
+            normed.at[:, columns(zl * 4 + xj, core)], lhs.at[pos, pl.ds(0, TOK)], load_sem.at[pos // 4]
         )
 
-    def partner_send(group, i):
-        zl, xj = block(group, i)
+    def partner_send(pos):
+        zl, xj = block(pos)
         return remote(
             normed.at[:, columns(zl * 4 + xj, other)],
-            lhs.at[before[group] + i, pl.ds(TOK, TOK)],
+            lhs.at[pos, pl.ds(TOK, TOK)],
             in_send.at[0],
-            in_recv.at[before[group] + i],
+            in_recv.at[pos],
             {"core": other},
         )
 
-    blocks = [(group, i) for group, count in enumerate(GROUPS) for i in range(count)]
-    grads_load = pltpu.make_async_copy(out_grads, rhs.at[pl.ds(0, TOK)], load_sem.at[len(GROUPS)])
+    grads_load = pltpu.make_async_copy(out_grads, rhs.at[pl.ds(0, TOK)], load_sem.at[4])
     grads_send = remote(out_grads, rhs.at[pl.ds(TOK, TOK)], in_send.at[1], in_recv.at[16], {"core": other})
 
     barrier = pltpu.get_barrier_semaphore()
@@ -259,12 +254,12 @@
     for device in neighbours:
         pl.semaphore_signal(barrier, inc=1, device_id=device, device_id_type=MESH_ID)
     grads_load.start()
-    for where in blocks:
-        own_load(*where).start()
+    for pos in range(16):
+        own_load(pos).start()
     pl.semaphore_wait(barrier, len(neighbours))
     grads_send.start()
-    for where in blocks:
-        partner_send(*where).start()
+    for pos in range(16):
+        partner_send(pos).start()
 
     sems = Sems(recv_sem)
     firsts = [sum(UNITS[:s]) for s in range(len(STREAMS))]
@@ -303,27 +298,22 @@
     grads_load.wait()
     grads_send.wait_recv()
 
-    def products(group):
-        first = before[group]
-        wait(lhs.at[pl.ds(first, GROUPS[group]), pl.ds(0, TOK)], load_sem.at[group])
-
-        def body(i, _):
-            partner_send(group, i).wait_recv()
-            zl, xj = block(group, i)
-            total = lax.dot_general(
-                lhs[first + i], rhs[...], (((0,), (0,)), ((), ())), preferred_element_type=F32
-            ).astype(BF16)
-            for yi in range(4):
-                for zh in range(2):
-                    at = {"x": xj, "y": yi, "z": zh * 4 + zl}
-                    rows = total[(yi * 2 + zh) * ROWS : (yi * 2 + zh + 1) * ROWS]
-                    for s, (a1, a2, a3) in enumerate(STREAMS):
-                        for u in range(UNITS[s]):
-                            place = (at[a1] * LENGTH[a2] + at[a2]) * LENGTH[a3] + at[a3]
-                            partials[s][place, u * 16 : u * 16 + 16] = rows[tile(s, u)]
-            return 0
-
-        lax.fori_loop(0, GROUPS[group], body, 0)
+    def product(pos):
+        if pos % 4 == 0:
+            wait(lhs.at[pl.ds(pos, 4), pl.ds(0, TOK)], load_sem.at[pos // 4])
+        partner_send(pos).wait_recv()
+        zl, xj = block(pos)
+        total = lax.dot_general(
+            lhs[pos], rhs[...], (((0,), (0,)), ((), ())), preferred_element_type=F32
+        ).astype(BF16)
+        for yi in range(4):
+            for zh in range(2):
+                at = {"x": xj, "y": yi, "z": zh * 4 + zl}
+                rows = total[(yi * 2 + zh) * ROWS : (yi * 2 + zh + 1) * ROWS]
+                for s, (a1, a2, a3) in enumerate(STREAMS):
+                    for u in range(UNITS[s]):
+                        place = (at[a1] * LENGTH[a2] + at[a2]) * LENGTH[a3] + at[a3]
+                        partials[s][place, u * 16 : u * 16 + 16] = rows[tile(s, u)]
 
     sums = jnp.zeros((8, 128), F32)
 
@@ -338,7 +328,7 @@
     rounds = [t for t in order if t[0] == "l" and t[2] == 0 and STREAMS[t[1]][0] == "z"]
     for t in order:
         if t[0] == "g":
-            products(t[1])
+            product(t[1])
         elif t[0] == "d":
             s, axis = t[1], STREAMS[t[1]][2]
             for off in FAR_FIRST[LENGTH[axis]][:-1]:
@@ -421,7 +411,7 @@
             pltpu.VMEM((2, 16, 128), F32),
             pltpu.SemaphoreType.DMA((many,)),
             pltpu.SemaphoreType.DMA((sems,)),
-            pltpu.SemaphoreType.DMA((len(GROUPS) + 1,)),
+            pltpu.SemaphoreType.DMA((5,)),
             pltpu.SemaphoreType.DMA((2,)),
             pltpu.SemaphoreType.DMA((17,)),
             pltpu.SemaphoreType.DMA((2, 2)),

time: 66 us -> 63.6 us (0.964)
  Pallas kernels: 64.4 us -> 62 us
    pallas_call x1, Pallas kernels: 64.4 us -> 62 us  [scaled_gradient(): pl.pallas_call(kernel, out_shape=pltpu.VMEM((ROWS, C), F32), in_specs=[pl...]
where the time goes in v4:
time: 63.6 us; the launch traced here: 63.5 us
  Pallas kernels  62 us (97%)
  other arithmetic  0.8 us (1%)
  between operations  0.69 us (1%)
    pallas_call x1, Pallas kernels, scaled_gradient(): pl.pallas_call(kernel, out_shape=pltpu.VMEM((ROWS, C), F32), in_specs=[pl...  62 us

profile of v4, /device:TPU:1, one launch (start us, length us, event | category | flops | bytes accessed | tf_op | source)
XLA Modules:
  0.0 63.5 jit_solution(10230017074024633749)
XLA Ops:
  0.6 0.0 copy-start.2
  0.6 0.0 copy-start.1
  0.7 0.0 copy-start
  0.7 62.0 %shard_map.76 = f32[32,1024]{1,0:T(8,128)S(1)} custom-call(bf16[256,8192]{1,0:T(8,128)(2,1)} %normed.1, bf16[256,1024]{1,0:T(8,128)(2,1)} %out_grads.1), custom_call_target="tpu_custom_call" | custom-call | tf_op jit(solution)/shard_map/pallas_call | solution.py:401
  62.7 0.0 copy-done.2
  62.7 0.0 copy-done.1
  62.7 0.0 copy-done
  62.7 0.8 %multiply_subtract_fusion = (f32[32,1024]{1,0:T(8,128)}, f32[32,1024]{1,0:T(8,128)}, f32[32,1024]{1,0:T(8,128)}) fusion(f32[32,1024]{1,0:T(8,128)S(1)} %copy-done, f32[32,1024]{1,0:T(8,128)S(1)} %shard_map.76, f32[32,1024]{1,0:T(8,128)S(1)} %copy-done.1, f32[32,1024]{1,0:T(8,128)S(1)} %copy-done.2), kind=kLoop, calls=%fused_computation.2 | loop fusion | flops 491520 | bytes 917504 | tf_op jit(solution)/shard_map/sub | solution.py:430
Async XLA Ops:
  0.6 62.1 %copy-start.2 = (f32[32,1024]{1,0:T(8,128)S(1)}, f32[32,1024]{1,0:T(8,128)}, u32[]{:S(2)}) copy-start(f32[32,1024]{1,0:T(8,128)} %param.9) | copy-start | bytes 393220
  0.6 62.1 %copy-start.1 = (f32[32,1024]{1,0:T(8,128)S(1)}, f32[32,1024]{1,0:T(8,128)}, u32[]{:S(2)}) copy-start(f32[32,1024]{1,0:T(8,128)} %param.8) | copy-start | bytes 393220
  0.7 62.1 %copy-start = (f32[32,1024]{1,0:T(8,128)S(1)}, f32[32,1024]{1,0:T(8,128)}, u32[]{:S(2)}) copy-start(f32[32,1024]{1,0:T(8,128)} %param.7) | copy-start | bytes 393220

commit v5 on v4

--- a/solution.py
+++ b/solution.py
@@ -21,7 +21,7 @@
     *((0, 2), (0, 3), (0, 1), (0, 0), (1, 2), (3, 3), (1, 1), (3, 0)),
     *((3, 2), (3, 1), (1, 3), (1, 0), (2, 2), (2, 3), (2, 1), (2, 0)),
 )
-PRODUCTS_FIRST, PRODUCTS_NEXT, RATE, LATE, ADDS, SLACK = 5.1, 0.47, 93.6e3, 2.0, 0.9e6, 3.0
+PRODUCTS_FIRST, PRODUCTS_NEXT, RATE, LATE, ADDS, SLACK = 5.1, 0.47, 93.6e3, 1.6, 0.9e6, 3.0
 
 
 def ring_length(s, k):
@@ -59,7 +59,7 @@
                 tasks += [("l", s, k, piece) for piece in range(piece_count(s, k))]
                 tasks += [("s", s, k, *which) for which in hops(s, k)]
             else:
-                tasks.append(("d", s))
+                tasks += [("d", s, 0), ("d", s, 1)]
     link, arrive, done, order = {}, {}, {}, []
 
     def size(s, k):
@@ -86,7 +86,7 @@
             return 0.0 if t[1] == 0 or ("g", t[1] - 1) in done else None
         came = []
         if t[0] == "d":
-            need = own(t[1], 2, 0, 0)
+            need = [("l", t[1], 1, t[2])]
         elif t[0] == "s":
             s, k, way, piece, hop = t[1:]
             n = ring_length(s, k)
@@ -279,7 +279,8 @@
             return ref.at[pl.ds(dest * n2 * n3 + n3 * i2, n3)]
 
         def second(dest, piece):
-            return ref.at[pl.ds(mine + n3 * dest + n3 // 2 * piece, n3 // 2)]
+            half = lax.rem(here[a3] // (n3 // 2) + 1 + piece, 2)
+            return ref.at[pl.ds(mine + n3 * dest + n3 // 2 * half, n3 // 2)]
 
         def third(dest, piece=0):
             return ref.at[pl.ds(mine + n3 * here[a2] + dest, 1)]
@@ -331,9 +332,10 @@
             product(t[1])
         elif t[0] == "d":
             s, axis = t[1], STREAMS[t[1]][2]
-            for off in FAR_FIRST[LENGTH[axis]][:-1]:
-                dest = lax.rem(here[axis] + off, LENGTH[axis])
-                landing = landings[2][s].at[off - 1]
+            at, odd = here[axis], lax.rem(here[axis], 2)
+            away = 2 - 2 * (at // 2)
+            for slot, dest in ((0, away + odd), (1, away + 1 - odd)) if t[2] == 0 else ((2, at + 1 - 2 * odd),):
+                landing = landings[2][s].at[slot]
                 remote(views(s)[2](dest), landing, send_sem.at[s], directs[s], place_of[axis](dest)).start()
         elif t[0] == "s":
             stages[t[1], t[2]].send(*t[3:])

time: 63.6 us -> 63.6 us (level)
  no operation moved by 1% of the time
where the time goes in v5:
time: 63.6 us; the launch traced here: 63.5 us
  Pallas kernels  62 us (97%)
  other arithmetic  0.8 us (1%)
  between operations  0.69 us (1%)
    pallas_call x1, Pallas kernels, scaled_gradient(): pl.pallas_call(kernel, out_shape=pltpu.VMEM((ROWS, C), F32), in_specs=[pl...  62 us

profile of v5, /device:TPU:1, one launch (start us, length us, event | category | flops | bytes accessed | tf_op | source)
XLA Modules:
  0.0 63.5 jit_solution(579150356793903405)
XLA Ops:
  0.6 0.0 copy-start.2
  0.6 0.0 copy-start.1
  0.7 0.0 copy-start
  0.7 62.0 %shard_map.76 = f32[32,1024]{1,0:T(8,128)S(1)} custom-call(bf16[256,8192]{1,0:T(8,128)(2,1)} %normed.1, bf16[256,1024]{1,0:T(8,128)(2,1)} %out_grads.1), custom_call_target="tpu_custom_call" | custom-call | tf_op jit(solution)/shard_map/pallas_call | solution.py:403
  62.7 0.0 copy-done.2
  62.7 0.0 copy-done.1
  62.7 0.0 copy-done
  62.7 0.8 %multiply_subtract_fusion = (f32[32,1024]{1,0:T(8,128)}, f32[32,1024]{1,0:T(8,128)}, f32[32,1024]{1,0:T(8,128)}) fusion(f32[32,1024]{1,0:T(8,128)S(1)} %copy-done, f32[32,1024]{1,0:T(8,128)S(1)} %shard_map.76, f32[32,1024]{1,0:T(8,128)S(1)} %copy-done.1, f32[32,1024]{1,0:T(8,128)S(1)} %copy-done.2), kind=kLoop, calls=%fused_computation.2 | loop fusion | flops 491520 | bytes 917504 | tf_op jit(solution)/shard_map/sub | solution.py:432
Async XLA Ops:
  0.6 62.1 %copy-start.2 = (f32[32,1024]{1,0:T(8,128)S(1)}, f32[32,1024]{1,0:T(8,128)}, u32[]{:S(2)}) copy-start(f32[32,1024]{1,0:T(8,128)} %param.9) | copy-start | bytes 393220
  0.6 62.1 %copy-start.1 = (f32[32,1024]{1,0:T(8,128)S(1)}, f32[32,1024]{1,0:T(8,128)}, u32[]{:S(2)}) copy-start(f32[32,1024]{1,0:T(8,128)} %param.8) | copy-start | bytes 393220
  0.7 62.1 %copy-start = (f32[32,1024]{1,0:T(8,128)S(1)}, f32[32,1024]{1,0:T(8,128)}, u32[]{:S(2)}) copy-start(f32[32,1024]{1,0:T(8,128)} %param.7) | copy-start | bytes 393220
